TPU v7x, 32 devices: a whole 2x2x4 slice. The times are simulated.
32 devices in a mesh: row: 4 (over y, x), col: 8 (over z, core).
Axes of the slice: x: 2, y: 2, z: 4, core: 2. Of those that a mesh axis runs over, the one named last changes fastest.
Arguments:
- activations: bfloat16 [512, 16384], P('col', 'row'), may hold values from -6 to 6
- grad_output: bfloat16 [512, 16384], P('col', 'row'), may hold values from -6 to 6
- gate_pre: bfloat16 [512, 8192], P('row', 'col'), may hold values from -8 to 8
- up_pre: bfloat16 [512, 8192], P('row', 'col'), may hold values from -6 to 6
- w_gate: bfloat16 [16384, 8192], P('row', 'col'), may hold values from -0.046875 to 0.046875
- w_up: bfloat16 [16384, 8192], P('row', 'col'), may hold values from -0.046875 to 0.046875
- w_down: bfloat16 [8192, 16384], P('col', 'row'), may hold values from -0.0625 to 0.0625
Outputs:
- grad_input: bfloat16 [512, 16384], P('col', 'row')
- grad_gate: bfloat16 [16384, 8192], P('row', 'col')
- grad_up: bfloat16 [16384, 8192], P('row', 'col')
- grad_down: bfloat16 [8192, 16384], P('col', 'row')
All inputs are finite; a program needn't handle non-finite values.
Results may differ from a plain program's by a relative error of at most 0.005.
Values may be sent and summed in bfloat16 or wider, within the bound.
A program may use at most 128 MiB of HBM per device.

v0:
```python
import jax
import jax.numpy as jnp
from jax import lax
from jax.sharding import PartitionSpec as P


def swiglu_grads(grad_hidden, gate_pre, up_pre):
    gate_val = gate_pre.astype(jnp.float32)
    up_val = up_pre.astype(jnp.float32)
    sigma = 1.0 / (1.0 + jnp.exp(-gate_val))
    grad_gate_pre = (grad_hidden * up_val * sigma * (1.0 + gate_val * (1.0 - sigma))).astype(
        jnp.bfloat16
    )
    grad_up_pre = (grad_hidden * gate_val * sigma).astype(jnp.bfloat16)
    return (grad_gate_pre, grad_up_pre)


def hidden_value(gate_pre, up_pre):
    gate_val = gate_pre.astype(jnp.float32)
    sigma = 1.0 / (1.0 + jnp.exp(-gate_val))
    return (gate_val * sigma * up_pre.astype(jnp.float32)).astype(jnp.bfloat16)


def local(activations, grad_output, gate_pre, up_pre, w_gate, w_up, w_down):
    contract_cols = (((1,), (1,)), ((), ()))
    contract_rows = (((0,), (0,)), ((), ()))
    acts_whole, grad_whole = (
        lax.all_gather(activations, "col", axis=0, tiled=True),
        lax.all_gather(grad_output, "col", axis=0, tiled=True),
    )
    gate_all, up_all = (
        lax.all_gather(gate_pre, "row", axis=0, tiled=True),
        lax.all_gather(up_pre, "row", axis=0, tiled=True),
    )
    partial_hidden = lax.dot_general(
        grad_whole, w_down, contract_cols, preferred_element_type=jnp.float32
    )
    grad_hidden = lax.psum(partial_hidden, "row")
    hidden_all = hidden_value(gate_all, up_all)
    gate_grad_all, up_grad_all = swiglu_grads(grad_hidden, gate_all, up_all)
    grad_down = lax.dot_general(
        hidden_all, grad_whole, contract_rows, preferred_element_type=jnp.float32
    ).astype(jnp.bfloat16)
    grad_gate = lax.dot_general(
        acts_whole, gate_grad_all, contract_rows, preferred_element_type=jnp.float32
    ).astype(jnp.bfloat16)
    grad_up = lax.dot_general(
        acts_whole, up_grad_all, contract_rows, preferred_element_type=jnp.float32
    ).astype(jnp.bfloat16)
    total = lax.dot_general(
        gate_grad_all, w_gate, contract_cols, preferred_element_type=jnp.float32
    )
    grad_input = lax.psum_scatter(
        total
        + lax.dot_general(up_grad_all, w_up, contract_cols, preferred_element_type=jnp.float32),
        "col",
        scatter_dimension=0,
        tiled=True,
    ).astype(jnp.bfloat16)
    return (grad_input, grad_gate, grad_up, grad_down)


def solution(mesh):
    in_specs = (
        P("col", "row"),
        P("col", "row"),
        P("row", "col"),
        P("row", "col"),
        P("row", "col"),
        P("row", "col"),
        P("col", "row"),
    )
    out_specs = (P("col", "row"), P("row", "col"), P("row", "col"), P("col", "row"))
    return jax.shard_map(local, mesh=mesh, in_specs=in_specs, out_specs=out_specs, check_vma=False)
```

profile of v0, /device:TPU:0, one launch (start us, length us, event | category | flops | bytes accessed | tf_op | source)
XLA Modules:
  0.0 335.6 jit_solution(11636700037328227497)
XLA Ops:
  7.2 0.0 all-gather.5.cloned.1.call-start
  7.2 0.7 all-gather.5.cloned.1.call-update
  7.9 0.0 all-gather.9.cloned.1.call-start
  7.9 0.7 all-gather.9.cloned.1.call-update
  8.6 0.0 all-gather.7.cloned.1.call-start
  8.7 0.7 all-gather.7.cloned.1.call-update
  9.4 0.0 all-reduce.2.cloned.1.call-start
  9.4 49.8 %all-gather.5.cloned.1.call-done = bf16[512,4096]{1,0:T(8,128)(2,1)} async-done(((bf16[64,4096]{1,0:T(8,128)(2,1)}), bf16[512,4096]{1,0:T(8,128)(2,1)}) %all-gather.5.cloned.1.call-update) | async-done | bytes 4194320 | tf_op jit(solution)/shard_map/all_gather | solution.py:29
  59.2 10.5 %fusion.15 = f32[512,1024]{1,0:T(8,128)} fusion(bf16[512,4096]{1,0:T(8,128)(2,1)} %all-gather.5.cloned.1.call-done, bf16[1024,4096]{1,0:T(8,128)(2,1)} %param.13), kind=kOutput, calls=%fused_computation.22 | convolution fusion | flops 4294967296 | bytes 14680064 | tf_op jit(solution)/shard_map/dot_general | solution.py:35
  69.7 0.0 all-reduce.2.cloned.1.call-update
  69.7 0.0 all-gather.11.cloned.1.call-start
  69.8 0.5 all-gather.11.cloned.1.call-update
  70.3 0.0 reduce-scatter.2.cloned.1.call-start
  70.4 16.0 %all-gather.9.cloned.1.call-done = bf16[512,1024]{1,0:T(8,128)(2,1)} async-done(((bf16[128,1024]{1,0:T(8,128)(2,1)}), bf16[512,1024]{1,0:T(8,128)(2,1)}) %all-gather.9.cloned.1.call-update) | async-done | bytes 1048592 | tf_op jit(solution)/shard_map/all_gather | solution.py:32
  86.4 28.4 %all-gather.7.cloned.1.call-done = bf16[512,1024]{1,0:T(8,128)(2,1)} async-done(((bf16[128,1024]{1,0:T(8,128)(2,1)}), bf16[512,1024]{1,0:T(8,128)(2,1)}) %all-gather.7.cloned.1.call-update) | async-done | bytes 1048592 | tf_op jit(solution)/shard_map/all_gather | solution.py:33
  114.8 73.0 %all-reduce.2.cloned.1.call-done = f32[512,1024]{1,0:T(8,128)} async-done(((f32[512,1024]{1,0:T(8,128)}), f32[512,1024]{1,0:T(8,128)}) %all-reduce.2.cloned.1.call-update) | async-done | bytes 2097168 | tf_op jit(solution)/shard_map/psum | solution.py:38
  187.8 3.1 fusion.2
  190.9 0.0 copy-start.2
  190.9 1.0 copy-done.2
  191.9 0.0 copy-start
  191.9 0.0 copy-start.1
  191.9 10.3 %fusion.16 = f32[512,4096]{1,0:T(8,128)} fusion(bf16[512,1024]{1,0:T(8,128)(2,1)S(1)} %fusion.2, bf16[4096,1024]{1,0:T(8,128)(2,1)} %param.11), kind=kOutput, calls=%fused_computation.23 | convolution fusion | flops 4294967296 | bytes 17825792 | tf_op jit(solution)/shard_map/dot_general | solution.py:50
  202.1 0.0 copy-done
  202.2 0.0 copy-done.1
  202.2 11.7 %convolution_add_fusion = f32[512,4096]{1,0:T(8,128)} fusion(f32[512,4096]{1,0:T(8,128)} %fusion.16, bf16[4096,1024]{1,0:T(8,128)(2,1)} %param.12, f32[512,1024]{1,0:T(8,128)S(1)} %copy-done, bf16[512,1024]{1,0:T(8,128)(2,1)S(1)} %copy-done.1), kind=kOutput, calls=%fused_computation.3 | convolution fusion | flops 4300734464 | bytes 28311552 | tf_op jit(solution)/shard_map/dot_general | solution.py:55
  213.8 0.0 reduce-scatter.2.cloned.1.call-update
  213.9 10.7 %convolution_convert_fusion = bf16[1024,4096]{1,0:T(8,128)(2,1)} fusion(bf16[512,4096]{1,0:T(8,128)(2,1)} %all-gather.5.cloned.1.call-done, bf16[512,1024]{1,0:T(8,128)(2,1)} %all-gather.7.cloned.1.call-done, bf16[512,1024]{1,0:T(8,128)(2,1)S(1)} %copy-done.1), kind=kOutput, calls=%fused_computation.2 | convolution fusion | flops 4303355904 | bytes 14680064 | tf_op jit(solution)/shard_map/dot_general | solution.py:41
  224.5 11.6 %all-gather.11.cloned.1.call-done = bf16[512,4096]{1,0:T(8,128)(2,1)} async-done(((bf16[64,4096]{1,0:T(8,128)(2,1)}), bf16[512,4096]{1,0:T(8,128)(2,1)}) %all-gather.11.cloned.1.call-update) | async-done | bytes 4194320 | tf_op jit(solution)/shard_map/all_gather | solution.py:28
  236.1 10.5 %convert_bitcast_fusion.1 = bf16[4096,1024]{0,1:T(8,128)(2,1)} fusion(bf16[512,1024]{1,0:T(8,128)(2,1)} %copy-done.2, bf16[512,4096]{1,0:T(8,128)(2,1)} %all-gather.11.cloned.1.call-done), kind=kOutput, calls=%fused_computation.1 | convolution fusion | flops 4299161600 | bytes 13631488 | tf_op jit(solution)/shard_map/dot_general | solution.py:44
  246.6 12.0 %copy.11 = bf16[4096,1024]{1,0:T(8,128)(2,1)} copy(bf16[4096,1024]{0,1:T(8,128)(2,1)} %convert_bitcast_fusion.1) | data formatting | bytes 16777216
  258.6 9.1 %convert_bitcast_fusion = bf16[4096,1024]{0,1:T(8,128)(2,1)} fusion(bf16[512,4096]{1,0:T(8,128)(2,1)} %all-gather.11.cloned.1.call-done, f32[512,1024]{1,0:T(8,128)S(1)} %copy-done, bf16[512,1024]{1,0:T(8,128)(2,1)S(1)} %copy-done.1), kind=kOutput, calls=%fused_computation | convolution fusion | flops 4302831616 | bytes 15728640 | tf_op jit(solution)/shard_map/dot_general | solution.py:47
  267.7 12.0 %copy.12 = bf16[4096,1024]{1,0:T(8,128)(2,1)} copy(bf16[4096,1024]{0,1:T(8,128)(2,1)} %convert_bitcast_fusion) | data formatting | bytes 16777216
  279.7 47.0 %reduce-scatter.2.cloned.1.call-done = f32[64,4096]{1,0:T(8,128)} async-done(((f32[512,4096]{1,0:T(8,128)}), f32[64,4096]{1,0:T(8,128)}) %reduce-scatter.2.cloned.1.call-update) | async-done | bytes 1048592 | tf_op jit(solution)/shard_map/reduce_scatter | solution.py:53
  326.7 2.1 convert_element_type.39
Async XLA Ops:
  7.2 52.0 %all-gather.5.cloned.1.call-start = ((), (), s32[]{:S(2)}) async-start(), calls=%async_computation.1 | async-start | bytes 4718592 | tf_op jit(solution)/shard_map/all_gather | solution.py:29
  7.9 78.5 %all-gather.9.cloned.1.call-start = ((), (), s32[]{:S(2)}) async-start(), calls=%async_computation.4 | async-start | bytes 1310720 | tf_op jit(solution)/shard_map/all_gather | solution.py:32
  8.6 106.1 %all-gather.7.cloned.1.call-start = ((), (), s32[]{:S(2)}) async-start(), calls=%async_computation.3 | async-start | bytes 1310720 | tf_op jit(solution)/shard_map/all_gather | solution.py:33
  9.4 178.4 %all-reduce.2.cloned.1.call-start = ((), (), s32[]{:S(2)}) async-start(), calls=%async_computation.2 | async-start | bytes 4194304 | tf_op jit(solution)/shard_map/psum | solution.py:38
  69.7 166.4 %all-gather.11.cloned.1.call-start = ((), (), s32[]{:S(2)}) async-start(), calls=%async_computation.6 | async-start | bytes 4718592 | tf_op jit(solution)/shard_map/all_gather | solution.py:28
  70.3 256.3 %reduce-scatter.2.cloned.1.call-start = ((), (), s32[]{:S(2)}) async-start(), calls=%async_computation.5 | async-start | bytes 9437184 | tf_op jit(solution)/shard_map/reduce_scatter | solution.py:53
  190.9 1.0 copy-start.2
  191.9 10.3 %copy-start = (f32[512,1024]{1,0:T(8,128)S(1)}, f32[512,1024]{1,0:T(8,128)}, u32[]{:S(2)}) copy-start(f32[512,1024]{1,0:T(8,128)} %all-reduce.2.cloned.1.call-done) | copy-start | bytes 6291460
  191.9 10.3 %copy-start.1 = (bf16[512,1024]{1,0:T(8,128)(2,1)S(1)}, bf16[512,1024]{1,0:T(8,128)(2,1)}, u32[]{:S(2)}) copy-start(bf16[512,1024]{1,0:T(8,128)(2,1)} %all-gather.9.cloned.1.call-done) | copy-start | bytes 3145732
Sparse Core Ops, SparseCore 0:
  9.6 49.5 all-gather.4
  61.0 25.2 all-gather.8
  88.2 26.4 all-gather.6
  118.3 69.4 all-reduce.1
  189.2 46.8 all-gather.10
  238.3 88.3 reduce-scatter.1
where the time goes:
time: 336 us
  waiting for transfers between devices  228 us (68%)
  matrix products  62.7 us (19%)
  local copies, waits for them, and re-layouts  24.9 us (7%)
  between operations  14.1 us (4%)
  other arithmetic  5.15 us (2%)
    psum x1, waiting for transfers between devices, local(): grad_hidden = lax.psum(partial_hidden, 'row')  73 us
    all_gather x1, waiting for transfers between devices, local(): lax.all_gather(grad_output, 'col', axis=0, tiled=True)  49.8 us
    reduce_scatter x1, waiting for transfers between devices, local(): lax.psum_scatter(total + lax.dot_general(up_grad_all, w_up, contract_cols...  47 us
    all_gather x1, waiting for transfers between devices, local(): lax.all_gather(up_pre, 'row', axis=0, tiled=True)  28.4 us
    unnamed x8, local copies, waits for them, and re-layouts  24.9 us
    all_gather x1, waiting for transfers between devices, local(): lax.all_gather(gate_pre, 'row', axis=0, tiled=True)  16 us
    dot_general x1, matrix products, local(): lax.dot_general(up_grad_all, w_up, contract_cols, preferred_element_type=...  11.7 us
    all_gather x1, waiting for transfers between devices, local(): lax.all_gather(activations, 'col', axis=0, tiled=True)  11.6 us
  transfers between devices with their start and end apart: 6, of which 6 were waited for; matrix products, arithmetic and copies ran while one was open for 27% of the time, Pallas kernels for 0%

commit v1 on v0

--- a/solution.py
+++ b/solution.py
@@ -35,7 +35,8 @@
     partial_hidden = lax.dot_general(
         grad_whole, w_down, contract_cols, preferred_element_type=jnp.float32
     )
-    grad_hidden = lax.psum(partial_hidden, "row")
+    parts = lax.all_gather(partial_hidden, "row")
+    grad_hidden = jnp.sum(parts, axis=0)
     hidden_all = hidden_value(gate_all, up_all)
     gate_grad_all, up_grad_all = swiglu_grads(grad_hidden, gate_all, up_all)
     grad_down = lax.dot_general(

time: 336 us -> 361 us (1.074)
  waiting for transfers between devices: 228 us -> 250 us
  other arithmetic: 5.15 us -> 9.08 us
    all_gather x0 -> x1, waiting for transfers between devices: none -> 84.5 us  [local(): parts = lax.all_gather(partial_hidden, 'row')]
    psum x1 -> x0, waiting for transfers between devices: 73 us -> none  [local(): grad_hidden = lax.psum(partial_hidden, 'row')]
    all_gather x1, waiting for transfers between devices: 16 us -> 23.8 us  [local(): lax.all_gather(gate_pre, 'row', axis=0, tiled=True)]
    reduce_sum x0 -> x1, other arithmetic: none -> 4.57 us  [local(): grad_hidden = jnp.sum(parts, axis=0)]
    unnamed x8 -> x6, local copies, waits for them, and re-layouts: 24.9 us -> 24.9 us
  transfers between devices with their start and end apart: 6 -> 6, of which waited for: 6 -> 6; matrix products, arithmetic and copies ran while one was open for 27% -> 23% of each run, Pallas kernels for 0% -> 0%
where the time goes in v1:
time: 361 us
  waiting for transfers between devices  250 us (69%)
  matrix products  62.7 us (17%)
  local copies, waits for them, and re-layouts  24.9 us (7%)
  between operations  14.1 us (4%)
  other arithmetic  9.08 us (3%)
    all_gather x1, waiting for transfers between devices, local(): parts = lax.all_gather(partial_hidden, 'row')  84.5 us
    all_gather x1, waiting for transfers between devices, local(): lax.all_gather(grad_output, 'col', axis=0, tiled=True)  51.3 us
    reduce_scatter x1, waiting for transfers between devices, local(): lax.psum_scatter(total + lax.dot_general(up_grad_all, w_up, contract_cols...  47 us
    all_gather x1, waiting for transfers between devices, local(): lax.all_gather(up_pre, 'row', axis=0, tiled=True)  28.2 us
    unnamed x6, local copies, waits for them, and re-layouts  24.9 us
    all_gather x1, waiting for transfers between devices, local(): lax.all_gather(gate_pre, 'row', axis=0, tiled=True)  23.8 us
    all_gather x1, waiting for transfers between devices, local(): lax.all_gather(activations, 'col', axis=0, tiled=True)  12.3 us
    dot_general x1, matrix products, local(): lax.dot_general(up_grad_all, w_up, contract_cols, preferred_element_type=...  11.6 us
  transfers between devices with their start and end apart: 6, of which 6 were waited for; matrix products, arithmetic and copies ran while one was open for 23% of the time, Pallas kernels for 0%

profile of v1, /device:TPU:0, one launch (start us, length us, event | category | flops | bytes accessed | tf_op | source)
XLA Modules:
  0.0 360.5 jit_solution(9212546418210119968)
XLA Ops:
  7.2 0.0 all-gather.7.cloned.1.call-start
  7.2 0.7 all-gather.7.cloned.1.call-update
  7.9 0.0 all-gather.15.cloned.1.call-start
  7.9 51.3 %all-gather.7.cloned.1.call-done = bf16[512,4096]{1,0:T(8,128)(2,1)} async-done(((bf16[64,4096]{1,0:T(8,128)(2,1)}), bf16[512,4096]{1,0:T(8,128)(2,1)}) %all-gather.7.cloned.1.call-update) | async-done | bytes 4194320 | tf_op jit(solution)/shard_map/all_gather | solution.py:29
  59.2 10.5 %fusion.15 = f32[512,1024]{1,0:T(8,128)} fusion(bf16[512,4096]{1,0:T(8,128)(2,1)} %all-gather.7.cloned.1.call-done, bf16[1024,4096]{1,0:T(8,128)(2,1)} %param.13), kind=kOutput, calls=%fused_computation.22 | convolution fusion | flops 4294967296 | bytes 14680064 | tf_op jit(solution)/shard_map/dot_general | solution.py:35
  69.7 0.0 all-gather.15.cloned.1.call-update
  69.7 0.0 all-gather.11.cloned.1.call-start
  69.8 0.7 all-gather.11.cloned.1.call-update
  70.5 0.0 all-gather.9.cloned.1.call-start
  70.5 0.5 all-gather.9.cloned.1.call-update
  71.0 0.0 all-gather.13.cloned.1.call-start
  71.1 0.5 all-gather.13.cloned.1.call-update
  71.6 0.0 reduce-scatter.2.cloned.1.call-start
  71.7 84.5 %all-gather.15.cloned.1.call-done = f32[2048,1024]{1,0:T(8,128)} async-done(((f32[512,1024]{1,0:T(8,128)}), f32[2048,1024]{1,0:T(8,128)}) %all-gather.15.cloned.1.call-update) | async-done | bytes 8388624 | tf_op jit(solution)/shard_map/all_gather | solution.py:38
  156.2 4.6 %reduce_sum.9 = f32[512,1024]{1,0:T(8,128)S(1)} reduce(f32[4,512,1024]{2,1,0:T(8,128)} %bitcast.14, f32[]{:T(128)} %constant.0.clone.1), dimensions={0}, to_apply=%region_0.0 | reduce | flops 1572864 | bytes 10485764 | tf_op jit(solution)/shard_map/reduce_sum | solution.py:39
  160.7 23.8 %all-gather.11.cloned.1.call-done = bf16[512,1024]{1,0:T(8,128)(2,1)} async-done(((bf16[128,1024]{1,0:T(8,128)(2,1)}), bf16[512,1024]{1,0:T(8,128)(2,1)}) %all-gather.11.cloned.1.call-update) | async-done | bytes 1048592 | tf_op jit(solution)/shard_map/all_gather | solution.py:32
  184.5 28.2 %all-gather.9.cloned.1.call-done = bf16[512,1024]{1,0:T(8,128)(2,1)} async-done(((bf16[128,1024]{1,0:T(8,128)(2,1)}), bf16[512,1024]{1,0:T(8,128)(2,1)}) %all-gather.9.cloned.1.call-update) | async-done | bytes 1048592 | tf_op jit(solution)/shard_map/all_gather | solution.py:33
  212.8 2.4 fusion.2
  215.2 0.0 copy-start.1
  215.2 1.0 copy-done.1
  216.2 0.0 copy-start
  216.2 10.2 %fusion.16 = f32[512,4096]{1,0:T(8,128)} fusion(bf16[512,1024]{1,0:T(8,128)(2,1)S(1)} %fusion.2, bf16[4096,1024]{1,0:T(8,128)(2,1)} %param.11), kind=kOutput, calls=%fused_computation.23 | convolution fusion | flops 4294967296 | bytes 17825792 | tf_op jit(solution)/shard_map/dot_general | solution.py:51
  226.4 0.0 copy-done
  226.4 11.6 %convolution_add_fusion = f32[512,4096]{1,0:T(8,128)} fusion(f32[512,4096]{1,0:T(8,128)} %fusion.16, bf16[4096,1024]{1,0:T(8,128)(2,1)} %param.12, f32[512,1024]{1,0:T(8,128)S(1)} %reduce_sum.9, bf16[512,1024]{1,0:T(8,128)(2,1)S(1)} %copy-done), kind=kOutput, calls=%fused_computation.3 | convolution fusion | flops 4300734464 | bytes 28311552 | tf_op jit(solution)/shard_map/dot_general | solution.py:56
  238.1 0.0 reduce-scatter.2.cloned.1.call-update
  238.1 10.7 %convolution_convert_fusion = bf16[1024,4096]{1,0:T(8,128)(2,1)} fusion(bf16[512,4096]{1,0:T(8,128)(2,1)} %all-gather.7.cloned.1.call-done, bf16[512,1024]{1,0:T(8,128)(2,1)} %all-gather.9.cloned.1.call-done, bf16[512,1024]{1,0:T(8,128)(2,1)S(1)} %copy-done), kind=kOutput, calls=%fused_computation.2 | convolution fusion | flops 4303355904 | bytes 14680064 | tf_op jit(solution)/shard_map/dot_general | solution.py:42
  248.8 12.3 %all-gather.13.cloned.1.call-done = bf16[512,4096]{1,0:T(8,128)(2,1)} async-done(((bf16[64,4096]{1,0:T(8,128)(2,1)}), bf16[512,4096]{1,0:T(8,128)(2,1)}) %all-gather.13.cloned.1.call-update) | async-done | bytes 4194320 | tf_op jit(solution)/shard_map/all_gather | solution.py:28
  261.1 10.5 %convert_bitcast_fusion.1 = bf16[4096,1024]{0,1:T(8,128)(2,1)} fusion(bf16[512,1024]{1,0:T(8,128)(2,1)} %copy-done.1, bf16[512,4096]{1,0:T(8,128)(2,1)} %all-gather.13.cloned.1.call-done), kind=kOutput, calls=%fused_computation.1 | convolution fusion | flops 4299161600 | bytes 13631488 | tf_op jit(solution)/shard_map/dot_general | solution.py:45
  271.6 12.0 %copy.11 = bf16[4096,1024]{1,0:T(8,128)(2,1)} copy(bf16[4096,1024]{0,1:T(8,128)(2,1)} %convert_bitcast_fusion.1) | data formatting | bytes 16777216
  283.5 9.1 %convert_bitcast_fusion = bf16[4096,1024]{0,1:T(8,128)(2,1)} fusion(bf16[512,4096]{1,0:T(8,128)(2,1)} %all-gather.13.cloned.1.call-done, f32[512,1024]{1,0:T(8,128)S(1)} %reduce_sum.9, bf16[512,1024]{1,0:T(8,128)(2,1)S(1)} %copy-done), kind=kOutput, calls=%fused_computation | convolution fusion | flops 4302831616 | bytes 15728640 | tf_op jit(solution)/shard_map/dot_general | solution.py:48
  292.7 12.0 %copy.12 = bf16[4096,1024]{1,0:T(8,128)(2,1)} copy(bf16[4096,1024]{0,1:T(8,128)(2,1)} %convert_bitcast_fusion) | data formatting | bytes 16777216
  304.6 47.0 %reduce-scatter.2.cloned.1.call-done = f32[64,4096]{1,0:T(8,128)} async-done(((f32[512,4096]{1,0:T(8,128)}), f32[64,4096]{1,0:T(8,128)}) %reduce-scatter.2.cloned.1.call-update) | async-done | bytes 1048592 | tf_op jit(solution)/shard_map/reduce_scatter | solution.py:54
  351.6 2.1 convert_element_type.39
Async XLA Ops:
  7.2 52.0 %all-gather.7.cloned.1.call-start = ((), (), s32[]{:S(2)}) async-start(), calls=%async_computation.1 | async-start | bytes 4718592 | tf_op jit(solution)/shard_map/all_gather | solution.py:29
  7.9 148.3 %all-gather.15.cloned.1.call-start = ((), (), s32[]{:S(2)}) async-start(), calls=%async_computation.6 | async-start | bytes 10485760 | tf_op jit(solution)/shard_map/all_gather | solution.py:38
  69.7 114.8 %all-gather.11.cloned.1.call-start = ((), (), s32[]{:S(2)}) async-start(), calls=%async_computation.3 | async-start | bytes 1310720 | tf_op jit(solution)/shard_map/all_gather | solution.py:32
  70.5 142.3 %all-gather.9.cloned.1.call-start = ((), (), s32[]{:S(2)}) async-start(), calls=%async_computation.2 | async-start | bytes 1310720 | tf_op jit(solution)/shard_map/all_gather | solution.py:33
  71.0 190.1 %all-gather.13.cloned.1.call-start = ((), (), s32[]{:S(2)}) async-start(), calls=%async_computation.5 | async-start | bytes 4718592 | tf_op jit(solution)/shard_map/all_gather | solution.py:28
  71.6 280.0 %reduce-scatter.2.cloned.1.call-start = ((), (), s32[]{:S(2)}) async-start(), calls=%async_computation.4 | async-start | bytes 9437184 | tf_op jit(solution)/shard_map/reduce_scatter | solution.py:54
  215.2 1.0 copy-start.1
  216.2 10.2 %copy-start = (bf16[512,1024]{1,0:T(8,128)(2,1)S(1)}, bf16[512,1024]{1,0:T(8,128)(2,1)}, u32[]{:S(2)}) copy-start(bf16[512,1024]{1,0:T(8,128)(2,1)} %all-gather.11.cloned.1.call-done) | copy-start | bytes 3145732
Sparse Core Ops, SparseCore 0:
  9.6 49.5 all-gather.6
  69.8 86.2 all-gather.14
  158.0 26.4 all-gather.10
  186.2 26.4 all-gather.8
  214.2 46.8 all-gather.12
  263.3 88.3 reduce-scatter.1
